TPU v7x, 32 devices: a whole 2x2x4 slice. The times are simulated.
32 devices in a mesh: blk: 8 (over z, core), fiber: 4 (over y, x).
Axes of the slice: x: 2, y: 2, z: 4, core: 2. Of those that a mesh axis runs over, the one named last changes fastest.
Arguments:
- embedding: bfloat16 [16384, 256], P(('blk', 'fiber')), may hold values from -2.09375 to 2.09375
- tile_dest: int32 [8, 4, 8, 24], P('blk', 'fiber'), may hold values from 0 to 15, as said below
- tile_source: int32 [8, 4, 8, 24], P('blk', 'fiber'), may hold values from 0 to 3
- tile_count: int32 [8, 4, 8], P('blk', 'fiber'), may hold values from 2 to 24, as said below
- pattern_id: int32 [8, 4, 8, 24], P('blk', 'fiber'), may hold values from 0 to 63
- pattern_bank: int32 [64, 4, 128], replicated, may hold values from -2147483648 to 2147483646
- negative_dest: int32 [8, 4, 8, 4], P('blk', 'fiber'), may hold values from 0 to 15
- negative_source: int32 [8, 4, 8, 4], P('blk', 'fiber'), may hold values from 0 to 3
Outputs:
- gradient: float32 [16384, 256], P(('blk', 'fiber'))
Inputs may be any that keep to these rules, and one draw needn't show every extreme that they name: At each block, fiber and stop the 24 pairs (tile_dest, tile_source) are distinct. `tile_count`: slots at or past the count are unused; some block, fiber and stop lists 24 tiles.
All inputs are finite; a program needn't handle non-finite values.
Results may differ from a plain program's by a relative error of at most 0.00064.
Values may be sent and summed in bfloat16 or wider, within the bound.
No kernel may reach another device: no remote copies, remote signals or barrier semaphores. Data moves between devices by JAX's collectives and lax.ppermute only.
A program may use at most 64 MiB of HBM per device.

v0:
```python
import functools

import jax
import jax.numpy as jnp
from jax import lax
from jax.experimental import pallas as pl
from jax.experimental.pallas import tpu as pltpu
from jax.sharding import PartitionSpec as P


LANES = 128
UNROLL = 3
COL_AT, MASK_AT = 8, 20
HALF_AT, STARTS_AT = 32, 64


def bank_kernel(bank_ref, out_ref):
    patterns, words, tile = bank_ref.shape
    shift = 31 - lax.broadcasted_iota(jnp.int32, (32, tile), 0)
    row = lax.broadcasted_iota(jnp.int32, (16, tile), 0)
    lane = lax.broadcasted_iota(jnp.int32, (16, tile), 1)
    in_row = (lane // 32 == row % words) & ((lane % 32) // 16 == row // words)
    weight = jnp.where(in_row, jnp.left_shift(1, lane % 16), 0).astype(jnp.float32).astype(jnp.bfloat16)
    out_ref[patterns] = jnp.zeros((words, tile), jnp.int32)
    out_ref[2 * patterns + 1] = jnp.zeros((words, tile), jnp.int32)

    def turn(pattern, _):
        packed = bank_ref[pattern]
        rows = [
            jnp.where(jnp.left_shift(packed[w : w + 1, :], shift) < 0, 1.0, 0.0)
            for w in range(words)
        ]
        bits = jnp.concatenate(rows, axis=0).astype(jnp.bfloat16)
        halves = lax.dot_general(
            weight, bits, (((1,), (1,)), ((), ())), preferred_element_type=jnp.float32
        ).astype(jnp.int32)
        out_ref[pattern] = packed
        out_ref[patterns + 1 + pattern] = halves[:words] + jnp.left_shift(
            halves[words : 2 * words], 16
        )
        return 0

    lax.fori_loop(0, patterns, turn, 0, unroll=16)


def turned_bank(pattern_bank):
    patterns, words, tile = pattern_bank.shape
    return pl.pallas_call(
        bank_kernel,
        out_shape=jax.ShapeDtypeStruct((2 * patterns + 2, words, tile), jnp.int32),
        in_specs=[pl.BlockSpec(memory_space=pltpu.VMEM)],
        out_specs=pl.BlockSpec(memory_space=pltpu.VMEM),
        cost_estimate=pl.CostEstimate(flops=10**8, bytes_accessed=10**6, transcendentals=0),
        compiler_params=pltpu.CompilerParams(vmem_limit_bytes=4 * 2**20),
        name="bank",
    )(pattern_bank)


def stage_kernel(columns, sub, blocks, first, patterns, *refs):
    shifts = sorted({dz for dz, _ in columns})
    flips = sorted({k for _, k in columns})
    refs = list(refs)
    place_ref = refs.pop(0)
    plane_refs = {k: refs.pop(0) for k in flips}
    ring_refs = {dz: refs.pop(0) for dz in shifts}
    column_refs = [refs.pop(0) for _ in columns]
    rows_ref = refs.pop(0)
    bank_ref = refs.pop(0)
    before_ref = None if first else refs.pop(0)
    acc_ref, held, scores, later_scores, residuals, later_residuals, work, waiting, sems = refs

    words, tile = bank_ref.shape[1:]
    copies = [
        pltpu.make_async_copy(ref.at[pl.ds(0, sub * tile)], held.at[pl.ds(at * sub * tile, sub * tile)], sems.at[at])
        for at, ref in enumerate(column_refs)
    ]
    for copy in copies:
        copy.start()
    if first:
        acc_ref[...] = jnp.zeros_like(acc_ref)
    else:
        acc_ref[...] = before_ref[...]
    empty = len(columns) * sub
    held[pl.ds(empty * tile, tile), :] = jnp.zeros((tile, held.shape[1]), held.dtype)
    nothing = (empty << COL_AT) + (patterns << MASK_AT)

    block = place_ref[0]
    fiber = place_ref[1]
    partner = place_ref[2]

    for own in range(2 * sub):
        waiting[own] = -1
    for step in range(4 * UNROLL):
        work[step] = 2 * sub + nothing

    def scan(line, at, owner, base, filled):
        def one(slot, filled):
            item = line[slot + at] + base
            own = item & 255
            earlier = waiting[own]
            work[filled] = earlier
            work[filled + 1] = item
            waiting[own] = jnp.where(earlier < 0, item, -1)
            return filled + jnp.where(earlier < 0, 0, 2)

        return lax.fori_loop(line[STARTS_AT + owner], line[STARTS_AT + 1 + owner], one, filled)

    filled = jnp.int32(4 * UNROLL)
    for at, (dz, k) in enumerate(columns):
        there = lax.rem(block + (blocks - 2 * dz), blocks)
        for r, mine in enumerate((block, partner)):
            stop = lax.rem(mine - there + blocks, blocks)
            base = r * sub + (at * sub << COL_AT) + (patterns + 1 << MASK_AT)
            filled = scan(plane_refs[k].at[r, stop], 0, fiber, base, filled)
            stop = lax.rem(there - mine + blocks, blocks)
            base = r * sub + (at * sub << COL_AT)
            filled = scan(ring_refs[dz].at[stop], HALF_AT, fiber ^ k, base, filled)
    for own in range(2 * sub):
        earlier = waiting[own]
        work[filled] = earlier
        work[filled + 1] = own + nothing
        filled += jnp.where(earlier < 0, 0, 2)
    for step in range(10 * UNROLL):
        work[filled + step] = 2 * sub + nothing

    for copy in copies:
        copy.wait()

    shift = 31 - lax.broadcasted_iota(jnp.int32, (32, tile), 0)

    def pair_at(index):
        items = work[index], work[index + 1]
        others = [
            held[pl.ds(pl.multiple_of(((item >> COL_AT) & 4095) * tile, tile), tile), :] for item in items
        ]
        return items, jnp.concatenate(others, axis=0)

    def signs(item):
        packed = bank_ref[item >> MASK_AT]
        return jnp.concatenate(
            [
                jnp.where(jnp.left_shift(packed[w : w + 1, :], shift) < 0, 1.0, -1.0)
                for w in range(words)
            ],
            axis=0,
        )

    def one_group(group, scored, scoring, ready, readying):
        for step in range(UNROLL):
            items, others = pair_at(2 * (group * UNROLL + step))
            acc_ref[items[0] & 255] += jnp.dot(ready[step], others, preferred_element_type=jnp.float32)
        for step in range(UNROLL):
            index = 2 * ((group + 1) * UNROLL + step)
            sign = jnp.concatenate([signs(work[index]), signs(work[index + 1])], axis=1)
            readying[step] = (sign - jnp.tanh(scored[step])).astype(jnp.bfloat16)
        for step in range(UNROLL):
            items, others = pair_at(2 * ((group + 2) * UNROLL + step))
            scoring[step] = lax.dot_general(
                rows_ref[items[0] & 255],
                others,
                (((1,), (1,)), ((), ())),
                preferred_element_type=jnp.float32,
            )

    def two_groups(step, _):
        one_group(2 * step, later_scores, scores, residuals, later_residuals)
        one_group(2 * step + 1, scores, later_scores, later_residuals, residuals)
        return 0

    lax.fori_loop(0, lax.div(filled + (4 * UNROLL - 1), 4 * UNROLL), two_groups, 0)


def stage(columns, place, planes, rings, arrays, rows, bank, acc, sub, blocks):
    tiles, tile, width = rows.shape
    patterns = bank.shape[0] // 2 - 1
    shifts = sorted({dz for dz, _ in columns})
    first = acc is None
    most = len(columns) * 4 * 2 * HALF_AT + 4 * tiles + 16 * UNROLL
    smem = pl.BlockSpec(memory_space=pltpu.SMEM)
    vmem = pl.BlockSpec(memory_space=pltpu.VMEM)
    operands = [place] + [planes[k] for k in sorted({k for _, k in columns})] + [rings[dz] for dz in shifts]
    specs = [smem] * len(operands)
    operands += list(arrays)
    specs += [pl.BlockSpec(memory_space=pl.ANY)] * len(arrays)
    operands += [rows, bank]
    specs += [vmem, vmem]
    if not first:
        operands.append(acc)
        specs.append(vmem)
    return pl.pallas_call(
        functools.partial(stage_kernel, columns, sub, blocks, first, patterns),
        out_shape=jax.ShapeDtypeStruct((tiles, tile, width), jnp.float32),
        in_specs=specs,
        out_specs=vmem,
        scratch_shapes=[
            pltpu.VMEM(((len(columns) * sub + 1) * tile, width), jnp.bfloat16),
            pltpu.VMEM((UNROLL, tile, 2 * tile), jnp.float32),
            pltpu.VMEM((UNROLL, tile, 2 * tile), jnp.float32),
            pltpu.VMEM((UNROLL, tile, 2 * tile), jnp.bfloat16),
            pltpu.VMEM((UNROLL, tile, 2 * tile), jnp.bfloat16),
            pltpu.SMEM((most,), jnp.int32),
            pltpu.SMEM((tiles,), jnp.int32),
            pltpu.SemaphoreType.DMA((len(columns),)),
        ],
        input_output_aliases={} if first else {len(operands) - 1: 0},
        cost_estimate=pl.CostEstimate(
            flops=len(columns) * 10**9, bytes_accessed=10**6, transcendentals=10**5
        ),
        compiler_params=pltpu.CompilerParams(vmem_limit_bytes=24 * 2**20),
        name="stage",
    )(*operands)


def parcel_kernel(sub, patterns, *refs):
    operands, (out_ref, lines_ref), held, sems = refs[:7], refs[7:9], refs[9:15], refs[15]
    count_ref, dest_ref, source_ref, mask_ref, away_ref, from_ref = held
    local_rows, width = operands[6].shape
    targets = list(held) + [out_ref.at[pl.ds(0, local_rows)]]
    copies = [
        pltpu.make_async_copy(ref, to, sems.at[n]) for n, (ref, to) in enumerate(zip(operands, targets))
    ]
    for copy in copies:
        copy.start()
    for copy in copies[:6]:
        copy.wait()
    stops, slots = dest_ref.shape[2:]
    negatives = away_ref.shape[2]
    row = lax.broadcasted_iota(jnp.int32, (stops, slots), 0)
    listed = lax.broadcasted_iota(jnp.int32, (stops, slots), 1)
    negative = lax.broadcasted_iota(jnp.int32, (stops, negatives), 1)
    negative_row = lax.broadcasted_iota(jnp.int32, (stops, negatives), 0)
    count = jnp.zeros((stops, slots), jnp.int32)
    away = jnp.zeros((stops, negatives), jnp.int32)
    away_source = jnp.zeros((stops, negatives), jnp.int32)
    for stop in range(stops):
        count = jnp.where(row == stop, count_ref[0, 0, stop], count)
        for k in range(negatives):
            here = (negative_row == stop) & (negative == k)
            away = jnp.where(here, away_ref[0, 0, k, stop], away)
            away_source = jnp.where(here, from_ref[0, 0, k, stop], away_source)
    dest = dest_ref[0, 0]
    owner = jnp.where(listed < count, dest // sub, LANES)
    away_owner = away // sub
    rank = jnp.zeros((stops, slots), jnp.int32)
    away_rank = jnp.zeros((stops, negatives), jnp.int32)
    one = lambda test: jnp.where(test, 1, 0)
    for k in range(slots):
        this = owner[:, k : k + 1]
        rank += one((this < owner) | ((this == owner) & (k < listed)))
        away_rank += one(this <= away_owner)
    for k in range(negatives):
        this = away_owner[:, k : k + 1]
        away_rank += one((this < away_owner) | ((this == away_owner) & (k < negative)))
        rank += one(this < owner)

    lane = lax.broadcasted_iota(jnp.int32, (stops, width), 1)
    at = lane % HALF_AT
    swapped = (lane // HALF_AT + lane // LANES) % 2 == 1
    which = jnp.zeros((stops, width), jnp.int32)
    masks = jnp.full((stops, width), patterns, jnp.int32)
    starts = jnp.zeros((stops, width), jnp.int32)
    tile, away_tile = dest % sub, away % sub
    source = source_ref[0, 0]
    mask = mask_ref[0, 0]
    for k in range(slots):
        col = slice(k, k + 1)
        here = at == rank[:, col]
        which = jnp.where(here, jnp.where(swapped, source[:, col], tile[:, col]), which)
        masks = jnp.where(here, mask[:, col], masks)
        starts += one(owner[:, col] < lane - STARTS_AT)
    for k in range(negatives):
        col = slice(k, k + 1)
        here = at == away_rank[:, col]
        which = jnp.where(here, jnp.where(swapped, away_source[:, col], away_tile[:, col]), which)
        masks = jnp.where(here, patterns, masks)
        starts += one(away_owner[:, col] < lane - STARTS_AT)
    which = jnp.where(lane % LANES < STARTS_AT, which, jnp.where(lane < LANES, starts, 0))
    masks = jnp.where(lane < STARTS_AT, masks, 0)
    lines = jnp.concatenate([which, masks], axis=0).astype(jnp.float32).astype(out_ref.dtype)
    out_ref[pl.ds(local_rows, 2 * stops), :] = lines
    lines_ref[...] = lines
    copies[6].wait()


def parcel_of(embedding, tile_dest, tile_source, tile_count, pattern_id, negative_dest, negative_source, tile, patterns):
    local_rows, width = embedding.shape
    stops = tile_dest.shape[2]
    operands = [
        tile_count,
        tile_dest,
        tile_source,
        pattern_id,
        jnp.swapaxes(negative_dest, 2, 3),
        jnp.swapaxes(negative_source, 2, 3),
    ]
    spaces = [pltpu.SMEM] + [pltpu.VMEM] * 3 + [pltpu.SMEM] * 2
    return pl.pallas_call(
        functools.partial(parcel_kernel, local_rows // tile, patterns),
        out_shape=[
            jax.ShapeDtypeStruct((local_rows + 2 * stops, width), embedding.dtype),
            jax.ShapeDtypeStruct((2 * stops, width), embedding.dtype),
        ],
        in_specs=[pl.BlockSpec(memory_space=pl.ANY)] * 7,
        out_specs=[pl.BlockSpec(memory_space=pltpu.VMEM)] * 2,
        scratch_shapes=[space(value.shape, jnp.int32) for space, value in zip(spaces, operands)]
        + [pltpu.SemaphoreType.DMA((7,))],
        cost_estimate=pl.CostEstimate(flops=10**8, bytes_accessed=10**6, transcendentals=0),
        compiler_params=pltpu.CompilerParams(vmem_limit_bytes=60 * 2**20),
        name="parcel",
    )(*operands, embedding)


def items_of(lines):
    lines = lines.astype(jnp.int32)
    stops = lines.shape[-2] // 2
    tiles, masks = lines[..., :stops, :], lines[..., stops:, :]
    return tiles[..., :LANES] + (tiles[..., LANES : 2 * LANES] << COL_AT) + (masks[..., :LANES] << MASK_AT)


def on_device(
    embedding, tile_dest, tile_source, tile_count, pattern_id, pattern_bank, negative_dest, negative_source
):
    local_rows, width = embedding.shape
    patterns, _, tile = pattern_bank.shape
    sub = local_rows // tile
    blocks = lax.axis_size("blk")
    fibers = lax.axis_size("fiber")
    ring = blocks // 2
    block = lax.axis_index("blk")
    fiber = lax.axis_index("fiber")

    def swap(value):
        return lax.ppermute(value, "blk", [(i, i ^ 1) for i in range(blocks)])

    def flip(value, k):
        return lax.ppermute(value, "fiber", [(i, i ^ k) for i in range(fibers)])

    def along(value, dz):
        return lax.ppermute(value, "blk", [(i, (i + 2 * dz) % blocks) for i in range(blocks)])

    parcel, lines = parcel_of(
        embedding,
        tile_dest,
        tile_source,
        tile_count,
        pattern_id,
        negative_dest,
        negative_source,
        tile,
        patterns,
    )
    place = jnp.stack([block, fiber, block ^ 1]).astype(jnp.int32)
    bank = turned_bank(pattern_bank)

    other = swap(parcel)
    got = {(0, 0): parcel}
    flips = range(1, fibers)
    bits = [1 << i for i in range(fibers.bit_length() - 1)]
    rest = [k for k in flips if k not in bits]
    for k in flips:
        got[0, k] = flip(parcel, k)
    got[1, 0] = along(parcel, 1)
    got[ring - 1, 0] = along(parcel, ring - 1)

    both = jnp.concatenate([embedding, other[:local_rows], jnp.zeros((tile, width), embedding.dtype)])
    rows = (both * jnp.asarray(0.5, embedding.dtype)).reshape(2 * sub + 1, tile, width)
    home = items_of(jnp.stack([lines, other[local_rows:]]))
    planes = {}
    for some in (bits, rest):
        plane = jnp.stack([got[0, k][local_rows:] for k in some])
        plane = items_of(jnp.stack([plane, swap(plane)]))
        planes |= {k: plane[:, at] for at, k in enumerate(some)}
    planes[0] = home
    rings = {0: home[0]}

    order = [1, ring - 1]
    for step in range(2, ring // 2 + 1):
        got[step, 0] = along(got[step - 1, 0], 1)
        order.append(step)
        if step != ring - step:
            got[ring - step, 0] = along(got[ring - step + 1, 0], ring - 1)
            order.append(ring - step)
    late = order[2:]
    for dz in order:
        rings[dz] = items_of(got[dz, 0][local_rows:])
        for k in bits:
            got[dz, k] = flip(got[dz, 0], k)
    for place_in, dz in enumerate(order):
        for k in rest:
            if place_in < 2:
                got[dz, k] = along(got[0, k], dz)
            else:
                got[dz, k] = flip(got[dz, 0], k)

    groups = [[(0, 0)], [(0, k) for k in bits], [(dz, 0) for dz in order[:2]]]
    groups.append([(0, k) for k in rest] + [(order[0], k) for k in bits])
    groups.append([(order[1], k) for k in bits] + [(dz, 0) for dz in late])
    groups.append([(dz, k) for dz in order[:2] for k in rest] + [(dz, k) for dz in late for k in flips])
    acc = None
    for columns in groups:
        acc = stage(columns, place, planes, rings, [got[c] for c in columns], rows, bank, acc, sub, blocks)
    total = acc[:sub] + swap(acc[sub : 2 * sub])
    scale = jnp.float32(0.5) / jnp.sqrt(jnp.float32(tile * blocks))
    return total.reshape(local_rows, width) * scale


def solution(mesh):
    listed = P("blk", "fiber", None, None)
    in_specs = (
        P(("blk", "fiber"), None),
        listed,
        listed,
        P("blk", "fiber", None),
        listed,
        P(),
        listed,
        listed,
    )

    return jax.shard_map(on_device, mesh=mesh, in_specs=in_specs, out_specs=P(("blk", "fiber"), None), check_vma=False)
```

profile of v0, /device:TPU:0, one launch (start us, length us, event | category | flops | bytes accessed | tf_op | source)
XLA Modules:
  0.0 72.6 jit_solution(14486863872679782547)
XLA Ops:
  0.0 1.9 %parcel.1 = (bf16[528,256]{1,0:T(8,128)(2,1)}, bf16[16,256]{1,0:T(8,128)(2,1)}) custom-call(s32[1,1,8]{2,1,0:T(1,128)} %refs_0_.1, s32[1,1,8,24]{3,2,1,0:T(8,128)} %refs_1_.1, s32[1,1,8,24]{3,2,1,0:T(8,128)} %refs_2_.1, s32[1,1,8,24]{3,2,1,0:T(8,128)} %refs_3_.1, s32[1,1,4,8]{3,2,1,0:T(4,128)} %bitcast.41, s32[1,1,4,8]{3,2,1,0:T(4,128)} %bitcast.42, ...), custom_call_target="tpu_custom_call" | custom-call | flops 100000000 | bytes 1000000 | tf_op jit(solution)/shard_map/parcel/pallas_call | solution.py:297
  2.0 0.6 collective-permute-start.13
  2.5 2.6 %collective-permute-start.1 = (bf16[528,256]{1,0:T(8,128)(2,1)}, bf16[528,256]{1,0:T(8,128)(2,1)S(1)}, u32[]{:S(2)}, u32[]{:S(2)}) collective-permute-start(bf16[528,256]{1,0:T(8,128)(2,1)} %get-tuple-element.7.refs_3_), channel_id=1, source_target_pairs={{0,2},{1,3},{2,0},{3,1},{4,6},{5,7},{6,4},{7,5},{8,10},{9,11},{10,... | collective-permute-start | bytes 811016 | tf_op jit(solution)/shard_map/ppermute | solution.py:336
  5.1 1.5 %collective-permute-start = (bf16[528,256]{1,0:T(8,128)(2,1)}, bf16[528,256]{1,0:T(8,128)(2,1)S(1)}, u32[]{:S(2)}, u32[]{:S(2)}) collective-permute-start(bf16[528,256]{1,0:T(8,128)(2,1)} %get-tuple-element.7.refs_3_), channel_id=1, source_target_pairs={{0,1},{1,0},{2,3},{3,2},{4,5},{5,4},{6,7},{7,6},{8,9},{9,8},{10,11... | collective-permute-start | bytes 811016 | tf_op jit(solution)/shard_map/ppermute | solution.py:336
  6.6 1.6 %collective-permute-start.5 = (bf16[528,256]{1,0:T(8,128)(2,1)}, bf16[528,256]{1,0:T(8,128)(2,1)S(1)}, u32[]{:S(2)}, u32[]{:S(2)}) collective-permute-start(bf16[528,256]{1,0:T(8,128)(2,1)} %get-tuple-element.7.refs_3_), channel_id=1, source_target_pairs={{0,8},{4,12},{8,16},{12,20},{16,24},{20,28},{24,0},{28,4},{1,9},{5... | collective-permute-start | bytes 811016 | tf_op jit(solution)/shard_map/ppermute | solution.py:339
  8.2 2.2 %collective-permute-start.7 = (bf16[528,256]{1,0:T(8,128)(2,1)}, bf16[528,256]{1,0:T(8,128)(2,1)S(1)}, u32[]{:S(2)}, u32[]{:S(2)}) collective-permute-start(bf16[528,256]{1,0:T(8,128)(2,1)} %get-tuple-element.7.refs_3_), channel_id=1, source_target_pairs={{0,24},{4,28},{8,0},{12,4},{16,8},{20,12},{24,16},{28,20},{1,25},{... | collective-permute-start | bytes 811016 | tf_op jit(solution)/shard_map/ppermute | solution.py:339
  10.4 0.9 %copy-done = s32[64,4,128]{2,1,0:T(4,128)S(1)} copy-done((s32[64,4,128]{2,1,0:T(4,128)S(1)}, s32[64,4,128]{2,1,0:T(4,128)}, u32[]{:S(2)}) %copy-start) | copy-done | bytes 131096
  11.3 1.6 %bank.1.refs_5_.refs_7_.refs_10_.refs_13_ = s32[130,4,128]{2,1,0:T(4,128)S(1)} custom-call(s32[64,4,128]{2,1,0:T(4,128)S(1)} %copy-done), custom_call_target="tpu_custom_call" | custom-call | flops 100000000 | bytes 1000000 | tf_op jit(solution)/shard_map/bank/pallas_call | solution.py:48
  12.9 0.1 pad_add_fusion.refs_0_
  13.0 0.0 collective-permute-done.13
  13.0 0.3 collective-permute-start.3
  13.3 0.7 fusion.4.refs_1_
  14.0 0.0 collective-permute-done.1.refs_5_
  14.0 0.0 collective-permute-done.refs_4_
  14.0 0.1 collective-permute-start.2
  14.1 3.9 %collective-permute-done.5.refs_4_ = bf16[528,256]{1,0:T(8,128)(2,1)S(1)} collective-permute-done((bf16[528,256]{1,0:T(8,128)(2,1)}, bf16[528,256]{1,0:T(8,128)(2,1)S(1)}, u32[]{:S(2)}, u32[]{:S(2)}) %collective-permute-start.5) | collective-permute-done | bytes 270368 | tf_op jit(solution)/shard_map/ppermute | solution.py:339
  18.0 4.1 %collective-permute-done.7.refs_5_ = bf16[528,256]{1,0:T(8,128)(2,1)S(1)} collective-permute-done((bf16[528,256]{1,0:T(8,128)(2,1)}, bf16[528,256]{1,0:T(8,128)(2,1)S(1)}, u32[]{:S(2)}, u32[]{:S(2)}) %collective-permute-start.7) | collective-permute-done | bytes 270368 | tf_op jit(solution)/shard_map/ppermute | solution.py:339
  22.2 0.0 collective-permute-done.3.refs_6_
  22.2 0.1 collective-permute-start.4
  22.3 0.2 maximum_multiply_fusion
  22.5 3.3 %stage.6.refs_8_ = f32[9,128,256]{2,1,0:T(8,128)S(1)} custom-call(s32[3]{0:T(128)S(1)} %pad_add_fusion.refs_0_, s32[2,8,128]{2,1,0:T(8,128)S(1)} %fusion.4.refs_1_, s32[8,128]{1,0:T(8,128)S(1)} %slice_bitcast_fusion.7.refs_2_.refs_3_.refs_4_, bf16[528,256]{1,0:T(8,128)(2,1)S(1)} %copy-done.1, bf16[9,128,256]{2,1,0:T(8,128)(2,1)S(1)} %bitcast.32, ...), custom_call_target="tpu_custom_call" | custom-call | flops 1000000000 | bytes 1000000 | tf_op jit(solution)/shard_map/stage/pallas_call | solution.py:190
  25.8 0.1 collective-permute-start.16
  25.9 0.4 collective-permute-start.17
  26.3 1.3 %collective-permute-start.6 = (bf16[528,256]{1,0:T(8,128)(2,1)S(1)}, bf16[528,256]{1,0:T(8,128)(2,1)S(1)}, u32[]{:S(2)}, u32[]{:S(2)}) collective-permute-start(bf16[528,256]{1,0:T(8,128)(2,1)S(1)} %collective-permute-done.5.refs_4_), channel_id=1, source_target_pairs={{0,8},{4,12},{8,16},{12,20},{16,24},{20,28},{24,0},{28,4},{1,9},{5... | collective-permute-start | bytes 811016 | tf_op jit(solution)/shard_map/ppermute | solution.py:339
  27.6 0.0 collective-permute-done.4
  27.6 1.4 %collective-permute-start.14 = (bf16[528,256]{1,0:T(8,128)(2,1)S(1)}, bf16[528,256]{1,0:T(8,128)(2,1)S(1)}, u32[]{:S(2)}, u32[]{:S(2)}) collective-permute-start(bf16[528,256]{1,0:T(8,128)(2,1)S(1)} %collective-permute-done.7.refs_5_), channel_id=1, source_target_pairs={{0,1},{1,0},{2,3},{3,2},{4,5},{5,4},{6,7},{7,6},{8,9},{9,8},{10,11... | collective-permute-start | bytes 811016 | tf_op jit(solution)/shard_map/ppermute | solution.py:336
  29.1 0.0 collective-permute-done.2
  29.1 1.5 %collective-permute-start.15 = (bf16[528,256]{1,0:T(8,128)(2,1)S(1)}, bf16[528,256]{1,0:T(8,128)(2,1)S(1)}, u32[]{:S(2)}, u32[]{:S(2)}) collective-permute-start(bf16[528,256]{1,0:T(8,128)(2,1)S(1)} %collective-permute-done.7.refs_5_), channel_id=1, source_target_pairs={{0,2},{1,3},{2,0},{3,1},{4,6},{5,7},{6,4},{7,5},{8,10},{9,11},{10,... | collective-permute-start | bytes 811016 | tf_op jit(solution)/shard_map/ppermute | solution.py:336
  30.6 4.2 %stage.7.refs_8_ = f32[9,128,256]{2,1,0:T(8,128)S(1)} custom-call(s32[3]{0:T(128)S(1)} %pad_add_fusion.refs_0_, s32[2,8,128]{2,1,0:T(8,128)S(1)} %get-tuple-element.12.refs_1_.refs_2_, s32[2,8,128]{2,1,0:T(8,128)S(1)} %get-tuple-element.11.refs_2_.refs_3_, s32[8,128]{1,0:T(8,128)S(1)} %slice_bitcast_fusion.7.refs_2_.refs_3_.refs_4_, ...), custom_call_target="tpu_custom_call", output_to_operand_aliasing={{}: (8, {})} | custom-call | flops 2000000000 | bytes 1000000 | tf_op jit(solution)/shard_map/stage/pallas_call | solution.py:190
  34.8 3.5 %stage.8.refs_11_ = f32[9,128,256]{2,1,0:T(8,128)S(1)} custom-call(s32[3]{0:T(128)S(1)} %pad_add_fusion.refs_0_, s32[2,8,128]{2,1,0:T(8,128)S(1)} %fusion.4.refs_1_, s32[8,128]{1,0:T(8,128)S(1)} %fusion.12.refs_2_.refs_5_.refs_4_, s32[8,128]{1,0:T(8,128)S(1)} %fusion.8.refs_3_.refs_5_.refs_6_, ...), custom_call_target="tpu_custom_call", output_to_operand_aliasing={{}: (8, {})} | custom-call | flops 2000000000 | bytes 1000000 | tf_op jit(solution)/shard_map/stage/pallas_call | solution.py:190
  38.4 0.0 collective-permute-done.6.refs_8_
  38.4 0.3 collective-permute-start.8
  38.7 0.0 collective-permute-done.16.refs_7_
  38.7 3.6 %collective-permute-start.9 = (bf16[528,256]{1,0:T(8,128)(2,1)S(1)}, bf16[528,256]{1,0:T(8,128)(2,1)S(1)}, u32[]{:S(2)}, u32[]{:S(2)}) collective-permute-start(bf16[528,256]{1,0:T(8,128)(2,1)S(1)} %collective-permute-done.3.refs_6_), channel_id=1, source_target_pairs={{0,24},{4,28},{8,0},{12,4},{16,8},{20,12},{24,16},{28,20},{1,25},{... | collective-permute-start | bytes 811016 | tf_op jit(solution)/shard_map/ppermute | solution.py:339
  42.3 0.0 collective-permute-done.17.refs_8_
  42.3 0.7 collective-permute-start.10
  43.0 5.2 %stage.9.refs_11_ = f32[9,128,256]{2,1,0:T(8,128)S(1)} custom-call(s32[3]{0:T(128)S(1)} %pad_add_fusion.refs_0_, s32[2,8,128]{2,1,0:T(8,128)S(1)} %get-tuple-element.12.refs_1_.refs_2_, s32[2,8,128]{2,1,0:T(8,128)S(1)} %get-tuple-element.11.refs_2_.refs_3_, s32[2,8,128]{2,1,0:T(8,128)S(1)} %fusion.7.refs_3_, ...), custom_call_target="tpu_custom_call", output_to_operand_aliasing={{}: (11, {})} | custom-call | flops 3000000000 | bytes 1000000 | tf_op jit(solution)/shard_map/stage/pallas_call | solution.py:190
  48.3 1.9 %collective-permute-start.11 = (bf16[528,256]{1,0:T(8,128)(2,1)S(1)}, bf16[528,256]{1,0:T(8,128)(2,1)S(1)}, u32[]{:S(2)}, u32[]{:S(2)}) collective-permute-start(bf16[528,256]{1,0:T(8,128)(2,1)S(1)} %collective-permute-done.6.refs_8_), channel_id=1, source_target_pairs={{0,2},{1,3},{2,0},{3,1},{4,6},{5,7},{6,4},{7,5},{8,10},{9,11},{10,... | collective-permute-start | bytes 811016 | tf_op jit(solution)/shard_map/ppermute | solution.py:336
  50.2 1.5 %collective-permute-start.12 = (bf16[528,256]{1,0:T(8,128)(2,1)S(1)}, bf16[528,256]{1,0:T(8,128)(2,1)S(1)}, u32[]{:S(2)}, u32[]{:S(2)}) collective-permute-start(bf16[528,256]{1,0:T(8,128)(2,1)S(1)} %collective-permute-done.6.refs_8_), channel_id=1, source_target_pairs={{0,3},{1,2},{2,1},{3,0},{4,7},{5,6},{6,5},{7,4},{8,11},{9,10},{10,... | collective-permute-start | bytes 811016 | tf_op jit(solution)/shard_map/ppermute | solution.py:336
  51.8 5.2 %stage.10.refs_14_ = f32[9,128,256]{2,1,0:T(8,128)S(1)} custom-call(s32[3]{0:T(128)S(1)} %pad_add_fusion.refs_0_, s32[2,8,128]{2,1,0:T(8,128)S(1)} %fusion.4.refs_1_, s32[2,8,128]{2,1,0:T(8,128)S(1)} %get-tuple-element.12.refs_1_.refs_2_, s32[2,8,128]{2,1,0:T(8,128)S(1)} %get-tuple-element.11.refs_2_.refs_3_, ...), custom_call_target="tpu_custom_call", output_to_operand_aliasing={{}: (11, {})} | custom-call | flops 3000000000 | bytes 1000000 | tf_op jit(solution)/shard_map/stage/pallas_call | solution.py:190
  57.0 0.0 collective-permute-done.9.refs_8_
  57.0 0.0 collective-permute-done.10.refs_9_
  57.0 3.9 %collective-permute-done.11.refs_10_ = bf16[528,256]{1,0:T(8,128)(2,1)S(1)} collective-permute-done((bf16[528,256]{1,0:T(8,128)(2,1)S(1)}, bf16[528,256]{1,0:T(8,128)(2,1)S(1)}, u32[]{:S(2)}, u32[]{:S(2)}) %collective-permute-start.11) | collective-permute-done | bytes 270368 | tf_op jit(solution)/shard_map/ppermute | solution.py:336
  61.0 0.0 collective-permute-done.12.refs_11_
  61.0 8.7 %stage.11 = f32[9,128,256]{2,1,0:T(8,128)S(1)} custom-call(s32[3]{0:T(128)S(1)} %pad_add_fusion.refs_0_, s32[2,8,128]{2,1,0:T(8,128)S(1)} %get-tuple-element.12.refs_1_.refs_2_, s32[2,8,128]{2,1,0:T(8,128)S(1)} %get-tuple-element.11.refs_2_.refs_3_, s32[2,8,128]{2,1,0:T(8,128)S(1)} %fusion.7.refs_3_, ...), custom_call_target="tpu_custom_call", output_to_operand_aliasing={{}: (14, {})} | custom-call | flops 5000000000 | bytes 1000000 | tf_op jit(solution)/shard_map/stage/pallas_call | solution.py:190
  69.7 0.1 collective-permute-start.18
  69.8 1.9 %collective-permute-done.18 = f32[4,128,256]{2,1,0:T(8,128)S(1)} collective-permute-done((f32[4,128,256]{2,1,0:T(8,128)S(1)}, f32[4,128,256]{2,1,0:T(8,128)S(1)}, u32[]{:S(2)}, u32[]{:S(2)}) %collective-permute-start.18) | collective-permute-done | bytes 524320 | tf_op jit(solution)/shard_map/ppermute | solution.py:333
  71.7 0.9 %fusion = f32[4,128,256]{2,1,0:T(8,128)} fusion(f32[4,128,256]{2,1,0:T(8,128)S(1)} %collective-permute-done.18, f32[9,128,256]{2,1,0:T(8,128)S(1)} %stage.11), kind=kLoop, calls=%fused_computation.2 | loop fusion | flops 262144 | bytes 1572864 | tf_op jit(solution)/shard_map/mul | solution.py:404
  (27 shorter events, 0.2 us)
Async XLA Ops:
  0.0 22.3 %copy-start.2 = (bf16[512,256]{1,0:T(8,128)(2,1)S(1)}, bf16[512,256]{1,0:T(8,128)(2,1)}, u32[]{:S(2)}) copy-start(bf16[512,256]{1,0:T(8,128)(2,1)} %refs_6_.1) | copy-start | bytes 786436
  2.0 11.0 %collective-permute-start.13 = (bf16[528,256]{1,0:T(8,128)(2,1)}, bf16[528,256]{1,0:T(8,128)(2,1)S(1)}, u32[]{:S(2)}, u32[]{:S(2)}) collective-permute-start(bf16[528,256]{1,0:T(8,128)(2,1)} %get-tuple-element.7.refs_3_), channel_id=1, source_target_pairs={{0,4},{4,0},{8,12},{12,8},{16,20},{20,16},{24,28},{28,24},{1,5},{5... | collective-permute-start | bytes 811016 | tf_op jit(solution)/shard_map/ppermute | solution.py:333
  2.5 11.5 %collective-permute-start.1 = (bf16[528,256]{1,0:T(8,128)(2,1)}, bf16[528,256]{1,0:T(8,128)(2,1)S(1)}, u32[]{:S(2)}, u32[]{:S(2)}) collective-permute-start(bf16[528,256]{1,0:T(8,128)(2,1)} %get-tuple-element.7.refs_3_), channel_id=1, source_target_pairs={{0,2},{1,3},{2,0},{3,1},{4,6},{5,7},{6,4},{7,5},{8,10},{9,11},{10,... | collective-permute-start | bytes 811016 | tf_op jit(solution)/shard_map/ppermute | solution.py:336
  5.1 8.9 %collective-permute-start = (bf16[528,256]{1,0:T(8,128)(2,1)}, bf16[528,256]{1,0:T(8,128)(2,1)S(1)}, u32[]{:S(2)}, u32[]{:S(2)}) collective-permute-start(bf16[528,256]{1,0:T(8,128)(2,1)} %get-tuple-element.7.refs_3_), channel_id=1, source_target_pairs={{0,1},{1,0},{2,3},{3,2},{4,5},{5,4},{6,7},{7,6},{8,9},{9,8},{10,11... | collective-permute-start | bytes 811016 | tf_op jit(solution)/shard_map/ppermute | solution.py:336
  6.6 11.4 %collective-permute-start.5 = (bf16[528,256]{1,0:T(8,128)(2,1)}, bf16[528,256]{1,0:T(8,128)(2,1)S(1)}, u32[]{:S(2)}, u32[]{:S(2)}) collective-permute-start(bf16[528,256]{1,0:T(8,128)(2,1)} %get-tuple-element.7.refs_3_), channel_id=1, source_target_pairs={{0,8},{4,12},{8,16},{12,20},{16,24},{20,28},{24,0},{28,4},{1,9},{5... | collective-permute-start | bytes 811016 | tf_op jit(solution)/shard_map/ppermute | solution.py:339
  8.2 14.0 %collective-permute-start.7 = (bf16[528,256]{1,0:T(8,128)(2,1)}, bf16[528,256]{1,0:T(8,128)(2,1)S(1)}, u32[]{:S(2)}, u32[]{:S(2)}) collective-permute-start(bf16[528,256]{1,0:T(8,128)(2,1)} %get-tuple-element.7.refs_3_), channel_id=1, source_target_pairs={{0,24},{4,28},{8,0},{12,4},{16,8},{20,12},{24,16},{28,20},{1,25},{... | collective-permute-start | bytes 811016 | tf_op jit(solution)/shard_map/ppermute | solution.py:339
  10.4 0.9 %copy-start = (s32[64,4,128]{2,1,0:T(4,128)S(1)}, s32[64,4,128]{2,1,0:T(4,128)}, u32[]{:S(2)}) copy-start(s32[64,4,128]{2,1,0:T(4,128)} %bank_ref.1) | copy-start | bytes 393220
  11.3 11.2 %copy-start.1 = (bf16[528,256]{1,0:T(8,128)(2,1)S(1)}, bf16[528,256]{1,0:T(8,128)(2,1)}, u32[]{:S(2)}) copy-start(bf16[528,256]{1,0:T(8,128)(2,1)} %get-tuple-element.7.refs_3_) | copy-start | bytes 811012
  13.0 9.2 %collective-permute-start.3 = (bf16[528,256]{1,0:T(8,128)(2,1)}, bf16[528,256]{1,0:T(8,128)(2,1)S(1)}, u32[]{:S(2)}, u32[]{:S(2)}) collective-permute-start(bf16[528,256]{1,0:T(8,128)(2,1)} %get-tuple-element.7.refs_3_), channel_id=1, source_target_pairs={{0,3},{1,2},{2,1},{3,0},{4,7},{5,6},{6,5},{7,4},{8,11},{9,10},{10,... | collective-permute-start | bytes 811016 | tf_op jit(solution)/shard_map/ppermute | solution.py:336
  14.0 15.0 %collective-permute-start.2 = (bf16[2,16,256]{2,1,0:T(8,128)(2,1)S(1)}, bf16[2,16,256]{2,1,0:T(8,128)(2,1)S(1)}, u32[]{:S(2)}, u32[]{:S(2)}) collective-permute-start(bf16[2,16,256]{2,1,0:T(8,128)(2,1)S(1)} %get-tuple-element.14), channel_id=1, source_target_pairs={{0,4},{4,0},{8,12},{12,8},{16,20},{20,16},{24,28},{28,24},{1,5},{5... | collective-permute-start | bytes 49160 | tf_op jit(solution)/shard_map/ppermute | solution.py:333
  22.2 5.4 %collective-permute-start.4 = (bf16[1,16,256]{2,1,0:T(8,128)(2,1)S(1)}, bf16[1,16,256]{2,1,0:T(8,128)(2,1)S(1)}, u32[]{:S(2)}, u32[]{:S(2)}) collective-permute-start(bf16[1,16,256]{2,1,0:T(8,128)(2,1)S(1)} %get-tuple-element.10), channel_id=1, source_target_pairs={{0,4},{4,0},{8,12},{12,8},{16,20},{20,16},{24,28},{28,24},{1,5},{5... | collective-permute-start | bytes 24584 | tf_op jit(solution)/shard_map/ppermute | solution.py:333
  25.8 12.8 %collective-permute-start.16 = (bf16[528,256]{1,0:T(8,128)(2,1)S(1)}, bf16[528,256]{1,0:T(8,128)(2,1)S(1)}, u32[]{:S(2)}, u32[]{:S(2)}) collective-permute-start(bf16[528,256]{1,0:T(8,128)(2,1)S(1)} %collective-permute-done.5.refs_4_), channel_id=1, source_target_pairs={{0,1},{1,0},{2,3},{3,2},{4,5},{5,4},{6,7},{7,6},{8,9},{9,8},{10,11... | collective-permute-start | bytes 811016 | tf_op jit(solution)/shard_map/ppermute | solution.py:336
  25.9 16.4 %collective-permute-start.17 = (bf16[528,256]{1,0:T(8,128)(2,1)S(1)}, bf16[528,256]{1,0:T(8,128)(2,1)S(1)}, u32[]{:S(2)}, u32[]{:S(2)}) collective-permute-start(bf16[528,256]{1,0:T(8,128)(2,1)S(1)} %collective-permute-done.5.refs_4_), channel_id=1, source_target_pairs={{0,2},{1,3},{2,0},{3,1},{4,6},{5,7},{6,4},{7,5},{8,10},{9,11},{10,... | collective-permute-start | bytes 811016 | tf_op jit(solution)/shard_map/ppermute | solution.py:336
  26.3 12.1 %collective-permute-start.6 = (bf16[528,256]{1,0:T(8,128)(2,1)S(1)}, bf16[528,256]{1,0:T(8,128)(2,1)S(1)}, u32[]{:S(2)}, u32[]{:S(2)}) collective-permute-start(bf16[528,256]{1,0:T(8,128)(2,1)S(1)} %collective-permute-done.5.refs_4_), channel_id=1, source_target_pairs={{0,8},{4,12},{8,16},{12,20},{16,24},{20,28},{24,0},{28,4},{1,9},{5... | collective-permute-start | bytes 811016 | tf_op jit(solution)/shard_map/ppermute | solution.py:339
  27.6 20.7 %collective-permute-start.14 = (bf16[528,256]{1,0:T(8,128)(2,1)S(1)}, bf16[528,256]{1,0:T(8,128)(2,1)S(1)}, u32[]{:S(2)}, u32[]{:S(2)}) collective-permute-start(bf16[528,256]{1,0:T(8,128)(2,1)S(1)} %collective-permute-done.7.refs_5_), channel_id=1, source_target_pairs={{0,1},{1,0},{2,3},{3,2},{4,5},{5,4},{6,7},{7,6},{8,9},{9,8},{10,11... | collective-permute-start | bytes 811016 | tf_op jit(solution)/shard_map/ppermute | solution.py:336
  29.1 21.1 %collective-permute-start.15 = (bf16[528,256]{1,0:T(8,128)(2,1)S(1)}, bf16[528,256]{1,0:T(8,128)(2,1)S(1)}, u32[]{:S(2)}, u32[]{:S(2)}) collective-permute-start(bf16[528,256]{1,0:T(8,128)(2,1)S(1)} %collective-permute-done.7.refs_5_), channel_id=1, source_target_pairs={{0,2},{1,3},{2,0},{3,1},{4,6},{5,7},{6,4},{7,5},{8,10},{9,11},{10,... | collective-permute-start | bytes 811016 | tf_op jit(solution)/shard_map/ppermute | solution.py:336
  38.4 18.6 %collective-permute-start.8 = (bf16[528,256]{1,0:T(8,128)(2,1)S(1)}, bf16[528,256]{1,0:T(8,128)(2,1)S(1)}, u32[]{:S(2)}, u32[]{:S(2)}) collective-permute-start(bf16[528,256]{1,0:T(8,128)(2,1)S(1)} %collective-permute-done.3.refs_6_), channel_id=1, source_target_pairs={{0,8},{4,12},{8,16},{12,20},{16,24},{20,28},{24,0},{28,4},{1,9},{5... | collective-permute-start | bytes 811016 | tf_op jit(solution)/shard_map/ppermute | solution.py:339
  38.7 18.3 %collective-permute-start.9 = (bf16[528,256]{1,0:T(8,128)(2,1)S(1)}, bf16[528,256]{1,0:T(8,128)(2,1)S(1)}, u32[]{:S(2)}, u32[]{:S(2)}) collective-permute-start(bf16[528,256]{1,0:T(8,128)(2,1)S(1)} %collective-permute-done.3.refs_6_), channel_id=1, source_target_pairs={{0,24},{4,28},{8,0},{12,4},{16,8},{20,12},{24,16},{28,20},{1,25},{... | collective-permute-start | bytes 811016 | tf_op jit(solution)/shard_map/ppermute | solution.py:339
  42.3 14.7 %collective-permute-start.10 = (bf16[528,256]{1,0:T(8,128)(2,1)S(1)}, bf16[528,256]{1,0:T(8,128)(2,1)S(1)}, u32[]{:S(2)}, u32[]{:S(2)}) collective-permute-start(bf16[528,256]{1,0:T(8,128)(2,1)S(1)} %collective-permute-done.6.refs_8_), channel_id=1, source_target_pairs={{0,1},{1,0},{2,3},{3,2},{4,5},{5,4},{6,7},{7,6},{8,9},{9,8},{10,11... | collective-permute-start | bytes 811016 | tf_op jit(solution)/shard_map/ppermute | solution.py:336
  48.3 12.7 %collective-permute-start.11 = (bf16[528,256]{1,0:T(8,128)(2,1)S(1)}, bf16[528,256]{1,0:T(8,128)(2,1)S(1)}, u32[]{:S(2)}, u32[]{:S(2)}) collective-permute-start(bf16[528,256]{1,0:T(8,128)(2,1)S(1)} %collective-permute-done.6.refs_8_), channel_id=1, source_target_pairs={{0,2},{1,3},{2,0},{3,1},{4,6},{5,7},{6,4},{7,5},{8,10},{9,11},{10,... | collective-permute-start | bytes 811016 | tf_op jit(solution)/shard_map/ppermute | solution.py:336
  50.2 10.7 %collective-permute-start.12 = (bf16[528,256]{1,0:T(8,128)(2,1)S(1)}, bf16[528,256]{1,0:T(8,128)(2,1)S(1)}, u32[]{:S(2)}, u32[]{:S(2)}) collective-permute-start(bf16[528,256]{1,0:T(8,128)(2,1)S(1)} %collective-permute-done.6.refs_8_), channel_id=1, source_target_pairs={{0,3},{1,2},{2,1},{3,0},{4,7},{5,6},{6,5},{7,4},{8,11},{9,10},{10,... | collective-permute-start | bytes 811016 | tf_op jit(solution)/shard_map/ppermute | solution.py:336
  69.7 2.0 %collective-permute-start.18 = (f32[4,128,256]{2,1,0:T(8,128)S(1)}, f32[4,128,256]{2,1,0:T(8,128)S(1)}, u32[]{:S(2)}, u32[]{:S(2)}) collective-permute-start(f32[4,128,256]{2,1,0:T(8,128)S(1)} %slice.175), channel_id=1, source_target_pairs={{0,4},{4,0},{8,12},{12,8},{16,20},{20,16},{24,28},{28,24},{1,5},{5... | collective-permute-start | bytes 1572872 | tf_op jit(solution)/shard_map/ppermute | solution.py:333
where the time goes:
time: 72.7 us; the launch traced here: 72.6 us
  Pallas kernels  33.7 us (46%)
  starting transfers between devices  21.7 us (30%)
  waiting for transfers between devices  13.9 us (19%)
  other arithmetic  1.93 us (3%)
  local copies, waits for them, and re-layouts  0.99 us (1%)
    pallas_call x6, Pallas kernels, stage(): pl.pallas_call(functools.partial(stage_kernel, columns, sub, blocks, firs...  30.2 us
    ppermute x10, starting transfers between devices, flip(): return lax.ppermute(value, 'fiber', [(i, i ^ k) for i in range(fibers)])  11.9 us
    ppermute x5, starting transfers between devices, along(): lax.ppermute(value, 'blk', [(i, (i + 2 * dz) % blocks) for i in range(blo...  9.03 us
    ppermute x5, waiting for transfers between devices, along(): lax.ppermute(value, 'blk', [(i, (i + 2 * dz) % blocks) for i in range(blo...  8.04 us
    ppermute x10, waiting for transfers between devices, flip(): return lax.ppermute(value, 'fiber', [(i, i ^ k) for i in range(fibers)])  3.97 us
    pallas_call x1, Pallas kernels, parcel_of(): pl.pallas_call(functools.partial(parcel_kernel, local_rows // tile, patte...  1.95 us
    ppermute x4, waiting for transfers between devices, swap(): return lax.ppermute(value, 'blk', [(i, i ^ 1) for i in range(blocks)])  1.9 us
    pallas_call x1, Pallas kernels, turned_bank(): pl.pallas_call(bank_kernel, out_shape=jax.ShapeDtypeStruct((2 * patterns...  1.57 us
  transfers between devices with their start and end apart: 19, of which 4 were waited for; matrix products, arithmetic and copies ran while one was open for 2% of the time, Pallas kernels for 32%

commit v1 on v0

--- a/solution.py
+++ b/solution.py
@@ -212,10 +212,10 @@
 
 
 def parcel_kernel(sub, patterns, *refs):
-    operands, (out_ref, lines_ref), held, sems = refs[:7], refs[7:9], refs[9:15], refs[15]
+    operands, (out_ref, lines_ref, bank_ref), held, sems = refs[:8], refs[8:11], refs[11:17], refs[17]
     count_ref, dest_ref, source_ref, mask_ref, away_ref, from_ref = held
     local_rows, width = operands[6].shape
-    targets = list(held) + [out_ref.at[pl.ds(0, local_rows)]]
+    targets = list(held) + [out_ref.at[pl.ds(0, local_rows)], bank_ref]
     copies = [
         pltpu.make_async_copy(ref, to, sems.at[n]) for n, (ref, to) in enumerate(zip(operands, targets))
     ]
@@ -279,11 +279,13 @@
     lines = jnp.concatenate([which, masks], axis=0).astype(jnp.float32).astype(out_ref.dtype)
     out_ref[pl.ds(local_rows, 2 * stops), :] = lines
     lines_ref[...] = lines
-    copies[6].wait()
-
-
-def parcel_of(embedding, tile_dest, tile_source, tile_count, pattern_id, negative_dest, negative_source, tile, patterns):
+    for copy in copies[6:]:
+        copy.wait()
+
+
+def parcel_of(embedding, tile_dest, tile_source, tile_count, pattern_id, negative_dest, negative_source, pattern_bank):
     local_rows, width = embedding.shape
+    patterns, _, tile = pattern_bank.shape
     stops = tile_dest.shape[2]
     operands = [
         tile_count,
@@ -299,15 +301,16 @@
         out_shape=[
             jax.ShapeDtypeStruct((local_rows + 2 * stops, width), embedding.dtype),
             jax.ShapeDtypeStruct((2 * stops, width), embedding.dtype),
+            jax.ShapeDtypeStruct(pattern_bank.shape, jnp.int32),
         ],
-        in_specs=[pl.BlockSpec(memory_space=pl.ANY)] * 7,
-        out_specs=[pl.BlockSpec(memory_space=pltpu.VMEM)] * 2,
+        in_specs=[pl.BlockSpec(memory_space=pl.ANY)] * 8,
+        out_specs=[pl.BlockSpec(memory_space=pltpu.VMEM)] * 3,
         scratch_shapes=[space(value.shape, jnp.int32) for space, value in zip(spaces, operands)]
-        + [pltpu.SemaphoreType.DMA((7,))],
+        + [pltpu.SemaphoreType.DMA((8,))],
         cost_estimate=pl.CostEstimate(flops=10**8, bytes_accessed=10**6, transcendentals=0),
         compiler_params=pltpu.CompilerParams(vmem_limit_bytes=60 * 2**20),
         name="parcel",
-    )(*operands, embedding)
+    )(*operands, embedding, pattern_bank)
 
 
 def items_of(lines):
@@ -321,7 +324,7 @@
     embedding, tile_dest, tile_source, tile_count, pattern_id, pattern_bank, negative_dest, negative_source
 ):
     local_rows, width = embedding.shape
-    patterns, _, tile = pattern_bank.shape
+    _, _, tile = pattern_bank.shape
     sub = local_rows // tile
     blocks = lax.axis_size("blk")
     fibers = lax.axis_size("fiber")
@@ -338,7 +341,7 @@
     def along(value, dz):
         return lax.ppermute(value, "blk", [(i, (i + 2 * dz) % blocks) for i in range(blocks)])
 
-    parcel, lines = parcel_of(
+    parcel, lines, pattern_bank = parcel_of(
         embedding,
         tile_dest,
         tile_source,
@@ -346,8 +349,7 @@
         pattern_id,
         negative_dest,
         negative_source,
-        tile,
-        patterns,
+        pattern_bank,
     )
     place = jnp.stack([block, fiber, block ^ 1]).astype(jnp.int32)
     bank = turned_bank(pattern_bank)
@@ -392,9 +394,8 @@
             else:
                 got[dz, k] = flip(got[dz, 0], k)
 
-    groups = [[(0, 0)], [(0, k) for k in bits], [(dz, 0) for dz in order[:2]]]
-    groups.append([(0, k) for k in rest] + [(order[0], k) for k in bits])
-    groups.append([(order[1], k) for k in bits] + [(dz, 0) for dz in late])
+    groups = [[(0, 0)], [(0, k) for k in bits]]
+    groups.append([(0, k) for k in rest] + [(dz, k) for dz in order[:2] for k in [0] + bits] + [(dz, 0) for dz in late])
     groups.append([(dz, k) for dz in order[:2] for k in rest] + [(dz, k) for dz in late for k in flips])
     acc = None
     for columns in groups:

time: 72.7 us -> 67.6 us (0.930)
  Pallas kernels: 33.7 us -> 30.5 us
  waiting for transfers between devices: 13.9 us -> 11.3 us
  starting transfers between devices: 21.7 us -> 22.5 us
    ppermute x5, waiting for transfers between devices: 8.04 us -> 3.86 us  [along(): lax.ppermute(value, 'blk', [(i, (i + 2 * dz) % blocks) for i in range(blo...]
    pallas_call x6 -> x4, Pallas kernels: 30.2 us -> 27 us  [stage(): pl.pallas_call(functools.partial(stage_kernel, columns, sub, blocks, firs...]
    ppermute x10, waiting for transfers between devices: 3.97 us -> 5.53 us  [flip(): return lax.ppermute(value, 'fiber', [(i, i ^ k) for i in range(fibers)])]
    ppermute x10, starting transfers between devices: 11.9 us -> 12.7 us  [flip(): return lax.ppermute(value, 'fiber', [(i, i ^ k) for i in range(fibers)])]
  transfers between devices with their start and end apart: 19 -> 19, of which waited for: 4 -> 6; matrix products, arithmetic and copies ran while one was open for 2% -> 2% of each run, Pallas kernels for 32% -> 29%
where the time goes in v1:
time: 67.6 us; the launch traced here: 67.5 us
  Pallas kernels  30.5 us (45%)
  starting transfers between devices  22.5 us (33%)
  waiting for transfers between devices  11.3 us (17%)
  other arithmetic  1.92 us (3%)
  local copies, waits for them, and re-layouts  0.99 us (1%)
    pallas_call x4, Pallas kernels, stage(): pl.pallas_call(functools.partial(stage_kernel, columns, sub, blocks, firs...  27 us
    ppermute x10, starting transfers between devices, flip(): return lax.ppermute(value, 'fiber', [(i, i ^ k) for i in range(fibers)])  12.7 us
    ppermute x5, starting transfers between devices, along(): lax.ppermute(value, 'blk', [(i, (i + 2 * dz) % blocks) for i in range(blo...  9.68 us
    ppermute x10, waiting for transfers between devices, flip(): return lax.ppermute(value, 'fiber', [(i, i ^ k) for i in range(fibers)])  5.53 us
    ppermute x5, waiting for transfers between devices, along(): lax.ppermute(value, 'blk', [(i, (i + 2 * dz) % blocks) for i in range(blo...  3.86 us
    pallas_call x1, Pallas kernels, parcel_of(): pl.pallas_call(functools.partial(parcel_kernel, local_rows // tile, patte...  1.98 us
    ppermute x4, waiting for transfers between devices, swap(): return lax.ppermute(value, 'blk', [(i, i ^ 1) for i in range(blocks)])  1.9 us
    pallas_call x1, Pallas kernels, turned_bank(): pl.pallas_call(bank_kernel, out_shape=jax.ShapeDtypeStruct((2 * patterns...  1.57 us
  transfers between devices with their start and end apart: 19, of which 6 were waited for; matrix products, arithmetic and copies ran while one was open for 2% of the time, Pallas kernels for 29%

profile of v1, /device:TPU:0, one launch (start us, length us, event | category | flops | bytes accessed | tf_op | source)
XLA Modules:
  0.0 67.5 jit_solution(9920618819271998321)
XLA Ops:
  0.0 2.0 %parcel.1 = (bf16[528,256]{1,0:T(8,128)(2,1)}, bf16[16,256]{1,0:T(8,128)(2,1)}, s32[64,4,128]{2,1,0:T(4,128)}) custom-call(s32[1,1,8]{2,1,0:T(1,128)} %refs_0_.1, s32[1,1,8,24]{3,2,1,0:T(8,128)} %refs_1_.1, s32[1,1,8,24]{3,2,1,0:T(8,128)} %refs_2_.1, s32[1,1,8,24]{3,2,1,0:T(8,128)} %refs_3_.1, s32[1,1,4,8]{3,2,1,0:T(4,128)} %bitcast.39, ...), custom_call_target="tpu_custom_call" | custom-call | flops 100000000 | bytes 1000000 | tf_op jit(solution)/shard_map/parcel/pallas_call | solution.py:299
  2.0 3.1 %collective-permute-start.1 = (bf16[528,256]{1,0:T(8,128)(2,1)}, bf16[528,256]{1,0:T(8,128)(2,1)S(1)}, u32[]{:S(2)}, u32[]{:S(2)}) collective-permute-start(bf16[528,256]{1,0:T(8,128)(2,1)} %get-tuple-element.8.refs_3_), channel_id=1, source_target_pairs={{0,2},{1,3},{2,0},{3,1},{4,6},{5,7},{6,4},{7,5},{8,10},{9,11},{10,... | collective-permute-start | bytes 811016 | tf_op jit(solution)/shard_map/ppermute | solution.py:339
  5.1 0.0 collective-permute-start.13
  5.1 1.5 %collective-permute-start = (bf16[528,256]{1,0:T(8,128)(2,1)}, bf16[528,256]{1,0:T(8,128)(2,1)S(1)}, u32[]{:S(2)}, u32[]{:S(2)}) collective-permute-start(bf16[528,256]{1,0:T(8,128)(2,1)} %get-tuple-element.8.refs_3_), channel_id=1, source_target_pairs={{0,1},{1,0},{2,3},{3,2},{4,5},{5,4},{6,7},{7,6},{8,9},{9,8},{10,11... | collective-permute-start | bytes 811016 | tf_op jit(solution)/shard_map/ppermute | solution.py:339
  6.6 0.1 collective-permute-start.3
  6.7 1.9 %collective-permute-start.5 = (bf16[528,256]{1,0:T(8,128)(2,1)}, bf16[528,256]{1,0:T(8,128)(2,1)S(1)}, u32[]{:S(2)}, u32[]{:S(2)}) collective-permute-start(bf16[528,256]{1,0:T(8,128)(2,1)} %get-tuple-element.8.refs_3_), channel_id=1, source_target_pairs={{0,8},{4,12},{8,16},{12,20},{16,24},{20,28},{24,0},{28,4},{1,9},{5... | collective-permute-start | bytes 811016 | tf_op jit(solution)/shard_map/ppermute | solution.py:342
  8.6 0.1 pad_add_fusion.refs_0_
  8.7 0.9 %copy-done = s32[64,4,128]{2,1,0:T(4,128)S(1)} copy-done((s32[64,4,128]{2,1,0:T(4,128)S(1)}, s32[64,4,128]{2,1,0:T(4,128)}, u32[]{:S(2)}) %copy-start) | copy-done | bytes 131096
  9.6 1.6 %bank.1.refs_5_.refs_7_.refs_18_.refs_13_ = s32[130,4,128]{2,1,0:T(4,128)S(1)} custom-call(s32[64,4,128]{2,1,0:T(4,128)S(1)} %copy-done), custom_call_target="tpu_custom_call" | custom-call | flops 100000000 | bytes 1000000 | tf_op jit(solution)/shard_map/bank/pallas_call | solution.py:48
  11.2 0.6 collective-permute-done.1.refs_5_
  11.7 3.8 %collective-permute-start.7 = (bf16[528,256]{1,0:T(8,128)(2,1)}, bf16[528,256]{1,0:T(8,128)(2,1)S(1)}, u32[]{:S(2)}, u32[]{:S(2)}) collective-permute-start(bf16[528,256]{1,0:T(8,128)(2,1)} %get-tuple-element.8.refs_3_), channel_id=1, source_target_pairs={{0,24},{4,28},{8,0},{12,4},{16,8},{20,12},{24,16},{28,20},{1,25},{... | collective-permute-start | bytes 811016 | tf_op jit(solution)/shard_map/ppermute | solution.py:342
  15.6 0.0 collective-permute-done.refs_4_
  15.6 0.1 collective-permute-start.2
  15.7 4.0 %collective-permute-done.3.refs_9_ = bf16[528,256]{1,0:T(8,128)(2,1)S(1)} collective-permute-done((bf16[528,256]{1,0:T(8,128)(2,1)}, bf16[528,256]{1,0:T(8,128)(2,1)S(1)}, u32[]{:S(2)}, u32[]{:S(2)}) %collective-permute-start.3) | collective-permute-done | bytes 270368 | tf_op jit(solution)/shard_map/ppermute | solution.py:339
  19.7 0.0 collective-permute-start.4
  19.7 0.0 collective-permute-done.13
  19.7 0.7 %fusion.4.refs_1_ = s32[2,8,128]{2,1,0:T(8,128)S(1)} fusion(bf16[1,16,256]{2,1,0:T(8,128)(2,1)S(1)} %slice_bitcast_fusion, bf16[1,16,256]{2,1,0:T(8,128)(2,1)} %bitcast.37), kind=kLoop, calls=%fused_computation.9 | loop fusion | flops 32768 | bytes 24576 | tf_op jit(solution)/shard_map/add | solution.py:320
  20.4 0.0 collective-permute-done.5.refs_10_
  20.4 2.9 %collective-permute-done.7.refs_13_ = bf16[528,256]{1,0:T(8,128)(2,1)S(1)} collective-permute-done((bf16[528,256]{1,0:T(8,128)(2,1)}, bf16[528,256]{1,0:T(8,128)(2,1)S(1)}, u32[]{:S(2)}, u32[]{:S(2)}) %collective-permute-start.7) | collective-permute-done | bytes 270368 | tf_op jit(solution)/shard_map/ppermute | solution.py:342
  23.3 0.2 maximum_multiply_fusion
  23.5 3.3 %stage.4.refs_8_ = f32[9,128,256]{2,1,0:T(8,128)S(1)} custom-call(s32[3]{0:T(128)S(1)} %pad_add_fusion.refs_0_, s32[2,8,128]{2,1,0:T(8,128)S(1)} %fusion.4.refs_1_, s32[8,128]{1,0:T(8,128)S(1)} %slice_bitcast_fusion.7.refs_2_.refs_3_.refs_5_, bf16[528,256]{1,0:T(8,128)(2,1)S(1)} %copy-done.1, bf16[9,128,256]{2,1,0:T(8,128)(2,1)S(1)} %bitcast.32, ...), custom_call_target="tpu_custom_call" | custom-call | flops 1000000000 | bytes 1000000 | tf_op jit(solution)/shard_map/stage/pallas_call | solution.py:190
  26.9 0.1 collective-permute-start.6
  27.0 2.0 %collective-permute-start.14 = (bf16[528,256]{1,0:T(8,128)(2,1)S(1)}, bf16[528,256]{1,0:T(8,128)(2,1)S(1)}, u32[]{:S(2)}, u32[]{:S(2)}) collective-permute-start(bf16[528,256]{1,0:T(8,128)(2,1)S(1)} %collective-permute-done.5.refs_10_), channel_id=1, source_target_pairs={{0,1},{1,0},{2,3},{3,2},{4,5},{5,4},{6,7},{7,6},{8,9},{9,8},{10,11... | collective-permute-start | bytes 811016 | tf_op jit(solution)/shard_map/ppermute | solution.py:339
  29.0 0.9 %collective-permute-start.15 = (bf16[528,256]{1,0:T(8,128)(2,1)S(1)}, bf16[528,256]{1,0:T(8,128)(2,1)S(1)}, u32[]{:S(2)}, u32[]{:S(2)}) collective-permute-start(bf16[528,256]{1,0:T(8,128)(2,1)S(1)} %collective-permute-done.5.refs_10_), channel_id=1, source_target_pairs={{0,2},{1,3},{2,0},{3,1},{4,6},{5,7},{6,4},{7,5},{8,10},{9,11},{10,... | collective-permute-start | bytes 811016 | tf_op jit(solution)/shard_map/ppermute | solution.py:339
  29.9 0.0 collective-permute-done.4
  29.9 0.6 collective-permute-start.16
  30.5 0.0 collective-permute-done.2
  30.5 0.7 collective-permute-start.17
  31.2 4.3 %stage.5.refs_19_ = f32[9,128,256]{2,1,0:T(8,128)S(1)} custom-call(s32[3]{0:T(128)S(1)} %pad_add_fusion.refs_0_, s32[2,8,128]{2,1,0:T(8,128)S(1)} %get-tuple-element.14.refs_1_.refs_2_, s32[2,8,128]{2,1,0:T(8,128)S(1)} %get-tuple-element.13.refs_2_.refs_3_, s32[8,128]{1,0:T(8,128)S(1)} %slice_bitcast_fusion.7.refs_2_.refs_3_.refs_5_, ...), custom_call_target="tpu_custom_call", output_to_operand_aliasing={{}: (8, {})} | custom-call | flops 2000000000 | bytes 1000000 | tf_op jit(solution)/shard_map/stage/pallas_call | solution.py:190
  35.5 1.0 %collective-permute-done.6.refs_16_ = bf16[528,256]{1,0:T(8,128)(2,1)S(1)} collective-permute-done((bf16[528,256]{1,0:T(8,128)(2,1)S(1)}, bf16[528,256]{1,0:T(8,128)(2,1)S(1)}, u32[]{:S(2)}, u32[]{:S(2)}) %collective-permute-start.6) | collective-permute-done | bytes 270368 | tf_op jit(solution)/shard_map/ppermute | solution.py:342
  36.5 0.0 collective-permute-start.8
  36.5 0.0 collective-permute-done.14.refs_11_
  36.5 3.9 %collective-permute-start.9 = (bf16[528,256]{1,0:T(8,128)(2,1)S(1)}, bf16[528,256]{1,0:T(8,128)(2,1)S(1)}, u32[]{:S(2)}, u32[]{:S(2)}) collective-permute-start(bf16[528,256]{1,0:T(8,128)(2,1)S(1)} %collective-permute-done.3.refs_9_), channel_id=1, source_target_pairs={{0,24},{4,28},{8,0},{12,4},{16,8},{20,12},{24,16},{28,20},{1,25},{... | collective-permute-start | bytes 811016 | tf_op jit(solution)/shard_map/ppermute | solution.py:342
  40.4 0.0 collective-permute-done.15.refs_12_
  40.4 2.2 %collective-permute-start.10 = (bf16[528,256]{1,0:T(8,128)(2,1)S(1)}, bf16[528,256]{1,0:T(8,128)(2,1)S(1)}, u32[]{:S(2)}, u32[]{:S(2)}) collective-permute-start(bf16[528,256]{1,0:T(8,128)(2,1)S(1)} %collective-permute-done.6.refs_16_), channel_id=1, source_target_pairs={{0,1},{1,0},{2,3},{3,2},{4,5},{5,4},{6,7},{7,6},{8,9},{9,8},{10,11... | collective-permute-start | bytes 811016 | tf_op jit(solution)/shard_map/ppermute | solution.py:339
  42.5 0.0 collective-permute-done.16.refs_14_
  42.6 1.5 %collective-permute-start.11 = (bf16[528,256]{1,0:T(8,128)(2,1)S(1)}, bf16[528,256]{1,0:T(8,128)(2,1)S(1)}, u32[]{:S(2)}, u32[]{:S(2)}) collective-permute-start(bf16[528,256]{1,0:T(8,128)(2,1)S(1)} %collective-permute-done.6.refs_16_), channel_id=1, source_target_pairs={{0,2},{1,3},{2,0},{3,1},{4,6},{5,7},{6,4},{7,5},{8,10},{9,11},{10,... | collective-permute-start | bytes 811016 | tf_op jit(solution)/shard_map/ppermute | solution.py:339
  44.0 0.0 collective-permute-done.17.refs_15_
  44.0 0.2 collective-permute-start.12
  44.2 10.5 %stage.6.refs_14_ = f32[9,128,256]{2,1,0:T(8,128)S(1)} custom-call(s32[3]{0:T(128)S(1)} %pad_add_fusion.refs_0_, s32[2,8,128]{2,1,0:T(8,128)S(1)} %fusion.4.refs_1_, s32[2,8,128]{2,1,0:T(8,128)S(1)} %get-tuple-element.14.refs_1_.refs_2_, s32[2,8,128]{2,1,0:T(8,128)S(1)} %get-tuple-element.13.refs_2_.refs_3_, ...), custom_call_target="tpu_custom_call", output_to_operand_aliasing={{}: (19, {})} | custom-call | flops 8000000000 | bytes 1000000 | tf_op jit(solution)/shard_map/stage/pallas_call | solution.py:190
  54.7 0.0 collective-permute-done.8.refs_7_
  54.7 0.0 collective-permute-done.9.refs_8_
  54.7 0.0 collective-permute-done.10.refs_9_
  54.7 0.9 %collective-permute-done.11.refs_10_ = bf16[528,256]{1,0:T(8,128)(2,1)S(1)} collective-permute-done((bf16[528,256]{1,0:T(8,128)(2,1)S(1)}, bf16[528,256]{1,0:T(8,128)(2,1)S(1)}, u32[]{:S(2)}, u32[]{:S(2)}) %collective-permute-start.11) | collective-permute-done | bytes 270368 | tf_op jit(solution)/shard_map/ppermute | solution.py:339
  55.7 8.9 %stage.7 = f32[9,128,256]{2,1,0:T(8,128)S(1)} custom-call(s32[3]{0:T(128)S(1)} %pad_add_fusion.refs_0_, s32[2,8,128]{2,1,0:T(8,128)S(1)} %get-tuple-element.14.refs_1_.refs_2_, s32[2,8,128]{2,1,0:T(8,128)S(1)} %get-tuple-element.13.refs_2_.refs_3_, s32[2,8,128]{2,1,0:T(8,128)S(1)} %fusion.7.refs_4_.refs_3_, ...), custom_call_target="tpu_custom_call", output_to_operand_aliasing={{}: (14, {})} | custom-call | flops 5000000000 | bytes 1000000 | tf_op jit(solution)/shard_map/stage/pallas_call | solution.py:190
  64.6 0.1 collective-permute-start.18
  64.7 1.9 %collective-permute-done.18 = f32[4,128,256]{2,1,0:T(8,128)S(1)} collective-permute-done((f32[4,128,256]{2,1,0:T(8,128)S(1)}, f32[4,128,256]{2,1,0:T(8,128)S(1)}, u32[]{:S(2)}, u32[]{:S(2)}) %collective-permute-start.18) | collective-permute-done | bytes 524320 | tf_op jit(solution)/shard_map/ppermute | solution.py:336
  66.6 0.9 %fusion = f32[4,128,256]{2,1,0:T(8,128)} fusion(f32[4,128,256]{2,1,0:T(8,128)S(1)} %collective-permute-done.18, f32[9,128,256]{2,1,0:T(8,128)S(1)} %stage.7), kind=kLoop, calls=%fused_computation.2 | loop fusion | flops 262144 | bytes 1572864 | tf_op jit(solution)/shard_map/mul | solution.py:405
  (25 shorter events, 0.2 us)
Async XLA Ops:
  0.0 23.3 %copy-start.2 = (bf16[512,256]{1,0:T(8,128)(2,1)S(1)}, bf16[512,256]{1,0:T(8,128)(2,1)}, u32[]{:S(2)}) copy-start(bf16[512,256]{1,0:T(8,128)(2,1)} %refs_6_.1) | copy-start | bytes 786436
  2.0 9.8 %collective-permute-start.1 = (bf16[528,256]{1,0:T(8,128)(2,1)}, bf16[528,256]{1,0:T(8,128)(2,1)S(1)}, u32[]{:S(2)}, u32[]{:S(2)}) collective-permute-start(bf16[528,256]{1,0:T(8,128)(2,1)} %get-tuple-element.8.refs_3_), channel_id=1, source_target_pairs={{0,2},{1,3},{2,0},{3,1},{4,6},{5,7},{6,4},{7,5},{8,10},{9,11},{10,... | collective-permute-start | bytes 811016 | tf_op jit(solution)/shard_map/ppermute | solution.py:339
  5.1 14.6 %collective-permute-start.13 = (bf16[528,256]{1,0:T(8,128)(2,1)}, bf16[528,256]{1,0:T(8,128)(2,1)S(1)}, u32[]{:S(2)}, u32[]{:S(2)}) collective-permute-start(bf16[528,256]{1,0:T(8,128)(2,1)} %get-tuple-element.8.refs_3_), channel_id=1, source_target_pairs={{0,4},{4,0},{8,12},{12,8},{16,20},{20,16},{24,28},{28,24},{1,5},{5... | collective-permute-start | bytes 811016 | tf_op jit(solution)/shard_map/ppermute | solution.py:336
  5.1 10.5 %collective-permute-start = (bf16[528,256]{1,0:T(8,128)(2,1)}, bf16[528,256]{1,0:T(8,128)(2,1)S(1)}, u32[]{:S(2)}, u32[]{:S(2)}) collective-permute-start(bf16[528,256]{1,0:T(8,128)(2,1)} %get-tuple-element.8.refs_3_), channel_id=1, source_target_pairs={{0,1},{1,0},{2,3},{3,2},{4,5},{5,4},{6,7},{7,6},{8,9},{9,8},{10,11... | collective-permute-start | bytes 811016 | tf_op jit(solution)/shard_map/ppermute | solution.py:339
  6.6 13.1 %collective-permute-start.3 = (bf16[528,256]{1,0:T(8,128)(2,1)}, bf16[528,256]{1,0:T(8,128)(2,1)S(1)}, u32[]{:S(2)}, u32[]{:S(2)}) collective-permute-start(bf16[528,256]{1,0:T(8,128)(2,1)} %get-tuple-element.8.refs_3_), channel_id=1, source_target_pairs={{0,3},{1,2},{2,1},{3,0},{4,7},{5,6},{6,5},{7,4},{8,11},{9,10},{10,... | collective-permute-start | bytes 811016 | tf_op jit(solution)/shard_map/ppermute | solution.py:339
  6.7 13.7 %collective-permute-start.5 = (bf16[528,256]{1,0:T(8,128)(2,1)}, bf16[528,256]{1,0:T(8,128)(2,1)S(1)}, u32[]{:S(2)}, u32[]{:S(2)}) collective-permute-start(bf16[528,256]{1,0:T(8,128)(2,1)} %get-tuple-element.8.refs_3_), channel_id=1, source_target_pairs={{0,8},{4,12},{8,16},{12,20},{16,24},{20,28},{24,0},{28,4},{1,9},{5... | collective-permute-start | bytes 811016 | tf_op jit(solution)/shard_map/ppermute | solution.py:342
  8.7 0.9 %copy-start = (s32[64,4,128]{2,1,0:T(4,128)S(1)}, s32[64,4,128]{2,1,0:T(4,128)}, u32[]{:S(2)}) copy-start(s32[64,4,128]{2,1,0:T(4,128)} %get-tuple-element.9.bank_ref) | copy-start | bytes 393220
  9.6 13.9 %copy-start.1 = (bf16[528,256]{1,0:T(8,128)(2,1)S(1)}, bf16[528,256]{1,0:T(8,128)(2,1)}, u32[]{:S(2)}) copy-start(bf16[528,256]{1,0:T(8,128)(2,1)} %get-tuple-element.8.refs_3_) | copy-start | bytes 811012
  11.7 11.5 %collective-permute-start.7 = (bf16[528,256]{1,0:T(8,128)(2,1)}, bf16[528,256]{1,0:T(8,128)(2,1)S(1)}, u32[]{:S(2)}, u32[]{:S(2)}) collective-permute-start(bf16[528,256]{1,0:T(8,128)(2,1)} %get-tuple-element.8.refs_3_), channel_id=1, source_target_pairs={{0,24},{4,28},{8,0},{12,4},{16,8},{20,12},{24,16},{28,20},{1,25},{... | collective-permute-start | bytes 811016 | tf_op jit(solution)/shard_map/ppermute | solution.py:342
  15.6 14.9 %collective-permute-start.2 = (bf16[2,16,256]{2,1,0:T(8,128)(2,1)S(1)}, bf16[2,16,256]{2,1,0:T(8,128)(2,1)S(1)}, u32[]{:S(2)}, u32[]{:S(2)}) collective-permute-start(bf16[2,16,256]{2,1,0:T(8,128)(2,1)S(1)} %get-tuple-element.16), channel_id=1, source_target_pairs={{0,4},{4,0},{8,12},{12,8},{16,20},{20,16},{24,28},{28,24},{1,5},{5... | collective-permute-start | bytes 49160 | tf_op jit(solution)/shard_map/ppermute | solution.py:336
  19.7 10.2 %collective-permute-start.4 = (bf16[1,16,256]{2,1,0:T(8,128)(2,1)S(1)}, bf16[1,16,256]{2,1,0:T(8,128)(2,1)S(1)}, u32[]{:S(2)}, u32[]{:S(2)}) collective-permute-start(bf16[1,16,256]{2,1,0:T(8,128)(2,1)S(1)} %get-tuple-element.12), channel_id=1, source_target_pairs={{0,4},{4,0},{8,12},{12,8},{16,20},{20,16},{24,28},{28,24},{1,5},{5... | collective-permute-start | bytes 24584 | tf_op jit(solution)/shard_map/ppermute | solution.py:336
  26.9 9.6 %collective-permute-start.6 = (bf16[528,256]{1,0:T(8,128)(2,1)S(1)}, bf16[528,256]{1,0:T(8,128)(2,1)S(1)}, u32[]{:S(2)}, u32[]{:S(2)}) collective-permute-start(bf16[528,256]{1,0:T(8,128)(2,1)S(1)} %collective-permute-done.5.refs_10_), channel_id=1, source_target_pairs={{0,8},{4,12},{8,16},{12,20},{16,24},{20,28},{24,0},{28,4},{1,9},{5... | collective-permute-start | bytes 811016 | tf_op jit(solution)/shard_map/ppermute | solution.py:342
  27.0 9.5 %collective-permute-start.14 = (bf16[528,256]{1,0:T(8,128)(2,1)S(1)}, bf16[528,256]{1,0:T(8,128)(2,1)S(1)}, u32[]{:S(2)}, u32[]{:S(2)}) collective-permute-start(bf16[528,256]{1,0:T(8,128)(2,1)S(1)} %collective-permute-done.5.refs_10_), channel_id=1, source_target_pairs={{0,1},{1,0},{2,3},{3,2},{4,5},{5,4},{6,7},{7,6},{8,9},{9,8},{10,11... | collective-permute-start | bytes 811016 | tf_op jit(solution)/shard_map/ppermute | solution.py:339
  29.0 11.4 %collective-permute-start.15 = (bf16[528,256]{1,0:T(8,128)(2,1)S(1)}, bf16[528,256]{1,0:T(8,128)(2,1)S(1)}, u32[]{:S(2)}, u32[]{:S(2)}) collective-permute-start(bf16[528,256]{1,0:T(8,128)(2,1)S(1)} %collective-permute-done.5.refs_10_), channel_id=1, source_target_pairs={{0,2},{1,3},{2,0},{3,1},{4,6},{5,7},{6,4},{7,5},{8,10},{9,11},{10,... | collective-permute-start | bytes 811016 | tf_op jit(solution)/shard_map/ppermute | solution.py:339
  29.9 12.7 %collective-permute-start.16 = (bf16[528,256]{1,0:T(8,128)(2,1)S(1)}, bf16[528,256]{1,0:T(8,128)(2,1)S(1)}, u32[]{:S(2)}, u32[]{:S(2)}) collective-permute-start(bf16[528,256]{1,0:T(8,128)(2,1)S(1)} %collective-permute-done.7.refs_13_), channel_id=1, source_target_pairs={{0,1},{1,0},{2,3},{3,2},{4,5},{5,4},{6,7},{7,6},{8,9},{9,8},{10,11... | collective-permute-start | bytes 811016 | tf_op jit(solution)/shard_map/ppermute | solution.py:339
  30.5 13.5 %collective-permute-start.17 = (bf16[528,256]{1,0:T(8,128)(2,1)S(1)}, bf16[528,256]{1,0:T(8,128)(2,1)S(1)}, u32[]{:S(2)}, u32[]{:S(2)}) collective-permute-start(bf16[528,256]{1,0:T(8,128)(2,1)S(1)} %collective-permute-done.7.refs_13_), channel_id=1, source_target_pairs={{0,2},{1,3},{2,0},{3,1},{4,6},{5,7},{6,4},{7,5},{8,10},{9,11},{10,... | collective-permute-start | bytes 811016 | tf_op jit(solution)/shard_map/ppermute | solution.py:339
  36.5 18.2 %collective-permute-start.8 = (bf16[528,256]{1,0:T(8,128)(2,1)S(1)}, bf16[528,256]{1,0:T(8,128)(2,1)S(1)}, u32[]{:S(2)}, u32[]{:S(2)}) collective-permute-start(bf16[528,256]{1,0:T(8,128)(2,1)S(1)} %collective-permute-done.3.refs_9_), channel_id=1, source_target_pairs={{0,8},{4,12},{8,16},{12,20},{16,24},{20,28},{24,0},{28,4},{1,9},{5... | collective-permute-start | bytes 811016 | tf_op jit(solution)/shard_map/ppermute | solution.py:342
  36.5 18.2 %collective-permute-start.9 = (bf16[528,256]{1,0:T(8,128)(2,1)S(1)}, bf16[528,256]{1,0:T(8,128)(2,1)S(1)}, u32[]{:S(2)}, u32[]{:S(2)}) collective-permute-start(bf16[528,256]{1,0:T(8,128)(2,1)S(1)} %collective-permute-done.3.refs_9_), channel_id=1, source_target_pairs={{0,24},{4,28},{8,0},{12,4},{16,8},{20,12},{24,16},{28,20},{1,25},{... | collective-permute-start | bytes 811016 | tf_op jit(solution)/shard_map/ppermute | solution.py:342
  40.4 14.4 %collective-permute-start.10 = (bf16[528,256]{1,0:T(8,128)(2,1)S(1)}, bf16[528,256]{1,0:T(8,128)(2,1)S(1)}, u32[]{:S(2)}, u32[]{:S(2)}) collective-permute-start(bf16[528,256]{1,0:T(8,128)(2,1)S(1)} %collective-permute-done.6.refs_16_), channel_id=1, source_target_pairs={{0,1},{1,0},{2,3},{3,2},{4,5},{5,4},{6,7},{7,6},{8,9},{9,8},{10,11... | collective-permute-start | bytes 811016 | tf_op jit(solution)/shard_map/ppermute | solution.py:339
  42.6 13.1 %collective-permute-start.11 = (bf16[528,256]{1,0:T(8,128)(2,1)S(1)}, bf16[528,256]{1,0:T(8,128)(2,1)S(1)}, u32[]{:S(2)}, u32[]{:S(2)}) collective-permute-start(bf16[528,256]{1,0:T(8,128)(2,1)S(1)} %collective-permute-done.6.refs_16_), channel_id=1, source_target_pairs={{0,2},{1,3},{2,0},{3,1},{4,6},{5,7},{6,4},{7,5},{8,10},{9,11},{10,... | collective-permute-start | bytes 811016 | tf_op jit(solution)/shard_map/ppermute | solution.py:339
  44.0 11.7 %collective-permute-start.12 = (bf16[528,256]{1,0:T(8,128)(2,1)S(1)}, bf16[528,256]{1,0:T(8,128)(2,1)S(1)}, u32[]{:S(2)}, u32[]{:S(2)}) collective-permute-start(bf16[528,256]{1,0:T(8,128)(2,1)S(1)} %collective-permute-done.6.refs_16_), channel_id=1, source_target_pairs={{0,3},{1,2},{2,1},{3,0},{4,7},{5,6},{6,5},{7,4},{8,11},{9,10},{10,... | collective-permute-start | bytes 811016 | tf_op jit(solution)/shard_map/ppermute | solution.py:339
  64.6 2.0 %collective-permute-start.18 = (f32[4,128,256]{2,1,0:T(8,128)S(1)}, f32[4,128,256]{2,1,0:T(8,128)S(1)}, u32[]{:S(2)}, u32[]{:S(2)}) collective-permute-start(f32[4,128,256]{2,1,0:T(8,128)S(1)} %slice.175), channel_id=1, source_target_pairs={{0,4},{4,0},{8,12},{12,8},{16,20},{20,16},{24,28},{28,24},{1,5},{5... | collective-permute-start | bytes 1572872 | tf_op jit(solution)/shard_map/ppermute | solution.py:336
